TPU v7x, 32 devices: a whole 2x2x4 slice. The times are simulated.
32 devices in a mesh: dp: 8 (over z, core), tensor: 4 (over y, x).
Axes of the slice: x: 2, y: 2, z: 4, core: 2. Of those that a mesh axis runs over, the one named last changes fastest.
Arguments:
- tokens: bfloat16 [18432, 2048], P(('dp', 'tensor')), may hold values from -6 to 6
- cotangent: bfloat16 [18432, 2048], P(('dp', 'tensor')), may hold values from -6 to 6
- ln_gain: float32 [2048], replicated, may hold values from 0.5 to 1.5
- ln_bias: float32 [2048], replicated, may hold values from -3 to 3
- w_qkv: bfloat16 [3, 2048, 2048], P(None, 'dp', 'tensor')
- b_qkv: float32 [3, 2048], P(None, 'tensor'), may hold values from -3 to 3
- w_out: bfloat16 [2048, 2048], P('tensor', 'dp'), may hold values from -0.5 to 0.5
- w_fc1: bfloat16 [2048, 8192], P('dp', 'tensor'), may hold values from -0.125 to 0.125
- b_fc1: float32 [8192], P('tensor'), may hold values from -3 to 3
- w_fc2: bfloat16 [8192, 2048], P('tensor', 'dp'), may hold values from -0.0625 to 0.0625
- resid_bias: float32 [2048], replicated, may hold values from -3 to 3
- parents: int32 [8, 18], P('dp'), may hold values from 0 to 9, as said below
Outputs:
- output_rows: bfloat16 [18432, 2048], P(('dp', 'tensor'))
- input_grad: float32 [18432, 2048], P(('dp', 'tensor'))
- grad_small: float32 [3, 2048], P(None, ('dp', 'tensor'))
- grad_w_qkv: float32 [3, 2048, 2048], P(None, 'dp', 'tensor')
- grad_b_qkv: float32 [3, 2048], P(None, 'tensor')
- grad_w_out: float32 [2048, 2048], P('tensor', 'dp')
- grad_w_fc1: float32 [2048, 8192], P('dp', 'tensor')
- grad_b_fc1: float32 [8192], P('tensor')
- grad_w_fc2: float32 [8192, 2048], P('tensor', 'dp')
- clipped_qk: bfloat16 [2, 2048, 2048], P(None, 'dp', 'tensor')
Inputs may be any that keep to these rules, and one draw needn't show every extreme that they name: `parents`: in each tree, segment 0 is its own parent and segment i < 6 has parent i - 1; the next 4 segments have parent 6 - 1; each of these is the parent of exactly 2 of the remaining segments.
All inputs are finite; a program needn't handle non-finite values.
Results may differ from a plain program's by a relative error of at most 0.014.
Values may be sent and summed in bfloat16 or wider, within the bound.
A program may use at most 384 MiB of HBM per device.

v0:
```python
import jax
import jax.numpy as jnp
from jax import lax
from jax.sharding import PartitionSpec as P

HDIM = 64
ROT = 32
SEG = 128
QBLK = 768
clip_tau = 10.0
norm_eps = 1e-05
rope_base = 10000.0


def tree_layout(parent_ids, seg_len):
    seg_count = parent_ids.shape[0]
    labels = jnp.arange(seg_count, dtype=jnp.int32)
    current = labels
    depth_seg = jnp.zeros((seg_count,), jnp.int32)
    ancestry = labels[:, None] == labels[None, :]
    for step_index in range(seg_count):
        depth_seg = depth_seg + (current != 0).astype(jnp.int32)
        current = jnp.sum(
            jnp.where(current[:, None] == labels[None, :], parent_ids[None, :], 0), axis=1
        )
        ancestry = ancestry | (current[:, None] == labels[None, :])
    positions = jnp.repeat(depth_seg, seg_len) * seg_len + jnp.tile(
        jnp.arange(seg_len, dtype=jnp.int32), seg_count
    )
    return (positions, ancestry)


def rotary_tables(positions):
    half_rot = ROT // 2
    inverse_freq = 1.0 / rope_base ** (jnp.arange(half_rot, dtype=jnp.float32) * (2.0 / ROT))
    angles = positions.astype(jnp.float32)[:, None] * inverse_freq[None, :]
    return (jnp.cos(angles), jnp.sin(angles))


def rotate(block_in, cos_rows, sin_rows):
    half_rot = ROT // 2
    first_half = block_in[..., :half_rot]
    second_half = block_in[..., half_rot:ROT]
    cos_heads = cos_rows[:, None, :]
    sin_heads = sin_rows[:, None, :]
    return jnp.concatenate(
        [
            first_half * cos_heads - second_half * sin_heads,
            second_half * cos_heads + first_half * sin_heads,
            block_in[..., ROT:],
        ],
        axis=-1,
    )


def unrotate(grad_in, cos_rows, sin_rows):
    half_rot = ROT // 2
    first_half = grad_in[..., :half_rot]
    second_half = grad_in[..., half_rot:ROT]
    cos_heads = cos_rows[:, None, :]
    sin_heads = sin_rows[:, None, :]
    return jnp.concatenate(
        [
            first_half * cos_heads + second_half * sin_heads,
            second_half * cos_heads - first_half * sin_heads,
            grad_in[..., ROT:],
        ],
        axis=-1,
    )


def block_mask(ancestry, row_start, row_count, total_rows, seg_len):
    row_ids = row_start + jnp.arange(row_count, dtype=jnp.int32)
    col_ids = jnp.arange(total_rows, dtype=jnp.int32)
    seg_rows = lax.dynamic_slice_in_dim(ancestry, row_start // seg_len, row_count // seg_len, 0)
    widened = jnp.repeat(jnp.repeat(seg_rows, seg_len, axis=0), seg_len, axis=1)
    same_seg = row_ids[:, None] // seg_len == col_ids[None, :] // seg_len
    return widened & (~same_seg | (col_ids[None, :] <= row_ids[:, None]))


def norm_rows(rows_in, gain_in, shift_in):
    row_mean = jnp.mean(rows_in, axis=-1, keepdims=True)
    centred = rows_in - row_mean
    inverse = lax.rsqrt(jnp.mean(centred * centred, axis=-1, keepdims=True) + norm_eps)
    return centred * inverse * gain_in + shift_in


def gelu_tanh(values_in):
    return jax.nn.gelu(values_in, approximate=True)


def body(
    tokens,
    cotangent,
    ln_gain,
    ln_bias,
    w_qkv,
    b_qkv,
    w_out,
    w_fc1,
    b_fc1,
    w_fc2,
    resid_bias,
    parents,
):
    local_rows = tokens.shape[0]
    total_rows = local_rows * lax.axis_size("tensor")
    own_start = lax.axis_index("tensor") * local_rows
    head_count = w_qkv.shape[2] // HDIM
    score_scale = HDIM ** (-0.5)
    positions, ancestry = tree_layout(parents[0], SEG)
    cos_rows, sin_rows = rotary_tables(positions)
    block_starts = jnp.arange(total_rows // QBLK, dtype=jnp.int32) * QBLK
    tokens_f = tokens.astype(jnp.float32)
    normed_local = norm_rows(tokens_f, ln_gain, ln_bias).astype(jnp.bfloat16)
    qkv_w, out_w, up_w, down_w = (
        lax.all_gather(w_qkv, "dp", axis=1, tiled=True),
        lax.all_gather(w_out, "dp", axis=1, tiled=True),
        lax.all_gather(w_fc1, "dp", axis=0, tiled=True),
        lax.all_gather(w_fc2, "dp", axis=1, tiled=True),
    )
    normed = lax.all_gather(normed_local, "tensor", axis=0, tiled=True)
    projected = (
        jnp.einsum("td,cdh->cth", normed, qkv_w, preferred_element_type=jnp.float32)
        + b_qkv[:, None, :]
    )
    heads_view = projected.reshape(3, total_rows, head_count, HDIM)
    queries = rotate(heads_view[0], cos_rows, sin_rows).astype(jnp.bfloat16)
    keys_rot = rotate(heads_view[1], cos_rows, sin_rows).astype(jnp.bfloat16)
    values_all = heads_view[2].astype(jnp.bfloat16)

    def attend_block(row_start):
        query_rows = lax.dynamic_slice_in_dim(queries, row_start, QBLK, 0)
        raw_scores = (
            jnp.einsum("qhe,khe->hqk", query_rows, keys_rot, preferred_element_type=jnp.float32)
            * score_scale
        )
        allowed = block_mask(ancestry, row_start, QBLK, total_rows, SEG)
        masked = jnp.where(allowed[None], raw_scores, -1e30)
        row_top = jnp.max(masked, axis=2)
        exponent = jnp.exp(masked - row_top[..., None])
        row_total = jnp.sum(exponent, axis=2)
        probs_low = (exponent / row_total[..., None]).astype(jnp.bfloat16)
        attended_rows = jnp.einsum(
            "hqk,khe->qhe", probs_low, values_all, preferred_element_type=jnp.float32
        ).astype(jnp.bfloat16)
        return (attended_rows, row_top + jnp.log(row_total), jnp.max(row_top, axis=1))

    attended, log_totals, block_tops = lax.map(attend_block, block_starts)
    attended = attended.reshape(total_rows, head_count * HDIM)
    hidden_pre = jnp.dot(normed, up_w, preferred_element_type=jnp.float32) + b_fc1
    activated = gelu_tanh(hidden_pre).astype(jnp.bfloat16)
    branch_whole = lax.psum(
        jnp.dot(attended, out_w, preferred_element_type=jnp.float32)
        + jnp.dot(activated, down_w, preferred_element_type=jnp.float32),
        "tensor",
    )
    branch_sum = lax.dynamic_slice_in_dim(branch_whole, own_start, local_rows, 0)
    output_rows = (tokens_f + branch_sum + resid_bias).astype(jnp.bfloat16)
    head_top = lax.pmax(jnp.max(block_tops, axis=0), "dp")
    factor = jnp.sqrt(clip_tau / jnp.maximum(head_top, clip_tau))
    clipped_qk = (w_qkv[:2].astype(jnp.float32) * jnp.repeat(factor, HDIM)[None, None, :]).astype(
        jnp.bfloat16
    )
    cot_full = lax.all_gather(cotangent, "tensor", axis=0, tiled=True)
    grad_attended = jnp.einsum(
        "td,hd->th", cot_full, out_w, preferred_element_type=jnp.float32
    ).astype(jnp.bfloat16)
    grad_w_out = jnp.einsum("th,td->hd", attended, cot_full, preferred_element_type=jnp.float32)
    grad_act = jnp.einsum("td,fd->tf", cot_full, down_w, preferred_element_type=jnp.float32)
    ignored, gelu_back = jax.vjp(gelu_tanh, hidden_pre)
    grad_hidden = gelu_back(grad_act)[0].astype(jnp.bfloat16)
    grad_w_fc2 = jnp.einsum("tf,td->fd", activated, cot_full, preferred_element_type=jnp.float32)
    grad_w_fc1 = jnp.einsum("td,tf->df", normed, grad_hidden, preferred_element_type=jnp.float32)
    grad_b_fc1 = jnp.sum(grad_hidden.astype(jnp.float32), axis=0)
    grad_heads = grad_attended.reshape(total_rows, head_count, HDIM)

    def back_block(carry, block_pair):
        grad_keys, grad_values = carry
        row_start, log_rows = block_pair
        query_rows = lax.dynamic_slice_in_dim(queries, row_start, QBLK, 0)
        grad_rows = lax.dynamic_slice_in_dim(grad_heads, row_start, QBLK, 0)
        raw_scores = (
            jnp.einsum("qhe,khe->hqk", query_rows, keys_rot, preferred_element_type=jnp.float32)
            * score_scale
        )
        allowed = block_mask(ancestry, row_start, QBLK, total_rows, SEG)
        masked = jnp.where(allowed[None], raw_scores, -1e30)
        probs_f = jnp.exp(masked - log_rows[..., None])
        probs_low = probs_f.astype(jnp.bfloat16)
        grad_probs = jnp.einsum(
            "qhe,khe->hqk", grad_rows, values_all, preferred_element_type=jnp.float32
        )
        grad_scores = (
            probs_f * (grad_probs - jnp.sum(probs_f * grad_probs, axis=2, keepdims=True))
        ).astype(jnp.bfloat16)
        grad_queries = (
            jnp.einsum("hqk,khe->qhe", grad_scores, keys_rot, preferred_element_type=jnp.float32)
            * score_scale
        )
        grad_keys = (
            grad_keys
            + jnp.einsum(
                "hqk,qhe->khe", grad_scores, query_rows, preferred_element_type=jnp.float32
            )
            * score_scale
        )
        grad_values = grad_values + jnp.einsum(
            "hqk,qhe->khe", probs_low, grad_rows, preferred_element_type=jnp.float32
        )
        return ((grad_keys, grad_values), grad_queries)

    zero_heads = jnp.zeros((total_rows, head_count, HDIM), jnp.float32)
    (grad_keys, grad_values), grad_queries = lax.scan(
        back_block, (zero_heads, zero_heads), (block_starts, log_totals)
    )
    grad_queries = grad_queries.reshape(total_rows, head_count, HDIM)
    grad_qkv = jnp.stack(
        [
            unrotate(grad_queries, cos_rows, sin_rows),
            unrotate(grad_keys, cos_rows, sin_rows),
            grad_values,
        ]
    )
    grad_qkv = grad_qkv.reshape(3, total_rows, head_count * HDIM).astype(jnp.bfloat16)
    grad_w_qkv = jnp.einsum("td,cth->cdh", normed, grad_qkv, preferred_element_type=jnp.float32)
    grad_b_qkv = jnp.sum(grad_qkv.astype(jnp.float32), axis=1)
    summed_qkv, summed_out, summed_fc1, summed_fc2 = (
        lax.psum_scatter(
            grad_w_qkv.astype(jnp.bfloat16), "dp", scatter_dimension=1, tiled=True
        ).astype(jnp.float32),
        lax.psum_scatter(
            grad_w_out.astype(jnp.bfloat16), "dp", scatter_dimension=1, tiled=True
        ).astype(jnp.float32),
        lax.psum_scatter(
            grad_w_fc1.astype(jnp.bfloat16), "dp", scatter_dimension=0, tiled=True
        ).astype(jnp.float32),
        lax.psum_scatter(
            grad_w_fc2.astype(jnp.bfloat16), "dp", scatter_dimension=1, tiled=True
        ).astype(jnp.float32),
    )
    bias_qkv, bias_fc1 = lax.psum((grad_b_qkv, grad_b_fc1), "dp")
    normed_all = lax.psum(
        (
            jnp.einsum("cth,cdh->td", grad_qkv, qkv_w, preferred_element_type=jnp.float32)
            + jnp.einsum("tf,df->td", grad_hidden, up_w, preferred_element_type=jnp.float32)
        ).astype(jnp.bfloat16),
        "tensor",
    ).astype(jnp.float32)
    grad_normed = lax.dynamic_slice_in_dim(normed_all, own_start, local_rows, 0)
    ignored_rows, norm_back = jax.vjp(norm_rows, tokens_f, ln_gain, ln_bias)
    grad_tokens, gain_part, shift_part = norm_back(grad_normed)
    cot_local = cotangent.astype(jnp.float32)
    input_grad = cot_local + grad_tokens
    small_terms = jnp.stack([gain_part, shift_part, jnp.sum(cot_local, axis=0)])
    grad_small = lax.psum_scatter(small_terms, ("dp", "tensor"), scatter_dimension=1, tiled=True)
    return (
        output_rows,
        input_grad,
        grad_small,
        summed_qkv,
        bias_qkv,
        summed_out,
        summed_fc1,
        bias_fc1,
        summed_fc2,
        clipped_qk,
    )


def solution(mesh):
    return jax.shard_map(
        body,
        mesh=mesh,
        in_specs=(
            P(("dp", "tensor"), None),
            P(("dp", "tensor"), None),
            P(),
            P(),
            P(None, "dp", "tensor"),
            P(None, "tensor"),
            P("tensor", "dp"),
            P("dp", "tensor"),
            P("tensor"),
            P("tensor", "dp"),
            P(),
            P("dp", None),
        ),
        out_specs=(
            P(("dp", "tensor"), None),
            P(("dp", "tensor"), None),
            P(None, ("dp", "tensor")),
            P(None, "dp", "tensor"),
            P(None, "tensor"),
            P("tensor", "dp"),
            P("dp", "tensor"),
            P("tensor"),
            P("tensor", "dp"),
            P(None, "dp", "tensor"),
        ),
        check_vma=False,
    )
```

profile of v0, /device:TPU:0, one launch (start us, length us, event | category | flops | bytes accessed | tf_op | source)
XLA Modules:
  0.0 2248.9 jit_solution(18235470847636643022)
XLA Ops:
  21.2 56.9 %all-gather.9.cloned.1.call-done = bf16[3,2048,512]{1,2,0:T(8,128)(2,1)} async-done(((bf16[3,256,512]{1,2,0:T(8,128)(2,1)}), bf16[3,2048,512]{1,2,0:T(8,128)(2,1)}) %all-gather.9.cloned.1.call-update) | async-done | bytes 6291472 | tf_op jit(solution)/shard_map/all_gather | solution.py:117
  78.1 96.4 %all-gather.7.cloned.1.call-done = bf16[2304,2048]{1,0:T(8,128)(2,1)} async-done(((bf16[576,2048]{1,0:T(8,128)(2,1)}), bf16[2304,2048]{1,0:T(8,128)(2,1)}) %all-gather.7.cloned.1.call-update) | async-done | bytes 9437200 | tf_op jit(solution)/shard_map/all_gather | solution.py:122
  207.6 261.1 %while.35 = (s32[]{:T(128)}, bf16[3,768,8,64]{1,3,2,0:T(8,128)(2,1)}, f32[3,8,768]{2,1,0:T(8,128)}, f32[3,8]{1,0:T(4,128)}, s32[3]{0:T(128)S(1)}, /*index=5*/pre...) while((s32[]{:T(128)}, ...), condition=%wide.region_24.25_spmd, body=%wide.region_20.24_spmd.sunk | while | flops 3817168896 | bytes 187103536 | solution.py:149
  229.4 25.1 %fusion.171 = (f32[8,768]{1,0:T(8,128)S(1)}, f32[8,768,2304]{2,1,0:T(8,128)}) fusion(pred[768,2304]{1,0:T(8,128)(4,1)S(1)} %copy.75, bf16[2304,8,64]{0,2,1:T(8,128)(2,1)} %get-tuple-element.657, bf16[2304,8,64]{0,2,1:T(8,128)(2,1)} %get-tuple-element.656, s32[]{:T(128)S(6)} %select_n.269), kind=kOutput, calls=%fused_computation.5.clone.1 | convolution fusion | flops 1854400512 | bytes 61562884 | tf_op jit(solution)/shard_map/while/body/eval_jaxpr/qhe,khe->hqk/dot_general | solution.py:135
  359.7 24.6 %fusion.173 = bf16[3,768,8,64]{1,3,2,0:T(8,128)(2,1)} fusion(bf16[3,768,8,64]{1,3,2,0:T(8,128)(2,1)} %get-tuple-element.634, s32[]{:T(128)} %get-tuple-element.633, bf16[2304,8,64]{0,2,1:T(8,128)(2,1)} %get-tuple-element.658, f32[8,768,2304]{2,1,0:T(8,128)} %get-tuple-element.597, f32[8,768]{1,0:T(8,128)S(1)} %get-tuple-element.599, ...), kind=kOutput, calls=%fused_computation.12.clone.1 | convolution fusion | flops 1883111424 | bytes 61587968 | tf_op jit(solution)/shard_map/while/body/eval_jaxpr/hqk,khe->qhe/dot_general | solution.py:144
  442.8 24.6 %fusion.173 = bf16[3,768,8,64]{1,3,2,0:T(8,128)(2,1)} fusion(bf16[3,768,8,64]{1,3,2,0:T(8,128)(2,1)} %get-tuple-element.634, s32[]{:T(128)} %get-tuple-element.633, bf16[2304,8,64]{0,2,1:T(8,128)(2,1)} %get-tuple-element.658, f32[8,768,2304]{2,1,0:T(8,128)} %get-tuple-element.597, f32[8,768]{1,0:T(8,128)S(1)} %get-tuple-element.599, ...), kind=kOutput, calls=%fused_computation.12.clone.1 | convolution fusion | flops 1883111424 | bytes 61587968 | tf_op jit(solution)/shard_map/while/body/eval_jaxpr/hqk,khe->qhe/dot_general | solution.py:144
  479.2 657.4 %while.36 = (s32[]{:T(128)}, f32[2304,8,64]{0,2,1:T(8,128)}, f32[2304,8,64]{0,2,1:T(8,128)}, f32[3,768,8,64]{1,0,3,2:T(4,128)}, s32[3]{0:T(128)S(1)}, /*index=5*...) while((s32[]{:T(128)}, f32[2304,8,64]{0,2,1:T(8,128)}, ...), condition=%wide.region_28.29_spmd.clone, body=%wide.region_26.28_spmd.clone.sunk | while | flops 9287196672 | bytes 472552672 | solution.py:214
  529.8 42.9 %multiply_reduce_fusion.2 = (f32[8,768]{1,0:T(8,128)S(1)}, f32[8,768,2304]{2,1,0:T(8,128)}) fusion(f32[8,768,2304]{2,1,0:T(8,128)} %fusion.183, f32[8,768]{1,0:T(8,128)S(1)} %dynamic-slice_bitcast_fusion.2, pred[768,2304]{1,0:T(8,128)(4,1)S(1)} %copy.77, bf16[2304,8,64]{0,2,1:T(8,128)(2,1)} %get-tuple-element.715, ...), kind=kOutput, calls=%fused_computation.38.clone.1 | convolution fusion | flops 1882712064 | bytes 118210560 | tf_op jit(solution)/shard_map/while/body/eval_jaxpr/qhe,khe->hqk/dot_general | solution.py:191
  572.7 44.8 %multiply_convert_fusion.6 = bf16[8,768,2304]{2,1,0:T(8,128)(2,1)} fusion(f32[8,768,2304]{2,1,0:T(8,128)} %get-tuple-element.614, f32[8,768,2304]{2,1,0:T(8,128)} %fusion.183, f32[8,768]{1,0:T(8,128)S(1)} %get-tuple-element.615, f32[8,768]{1,0:T(8,128)S(1)} %dynamic-slice_bitcast_fusion.2, pred[768,2304]{1,0:T(8,128)(4,1)S(1)} %copy.77), kind=kLoop, calls=%fused_computation.37.clone.1 | loop fusion | flops 84934656 | bytes 143376384 | tf_op jit(solution)/shard_map/while/body/eval_jaxpr/convert_element_type | solution.py:196
  634.2 30.3 %dynamic_update_slice.42 = f32[3,768,8,64]{1,0,3,2:T(4,128)} dynamic-update-slice(f32[3,768,8,64]{1,0,3,2:T(4,128)} %get-tuple-element.689, f32[1,768,8,64]{1,0,3,2:T(1,128)} %copy.78, s32[]{:T(128)} %get-tuple-element.686, s32[]{:T(128)} %constant.247.clone.1..sunk.1, s32[]{:T(128)} %constant.247.clone.1..sunk.1, s32[]{:T(128)} %constant.247.clone.1..sunk.1) | dynamic-update-slice | bytes 3145732 | tf_op jit(solution)/shard_map/while/body/jit(dynamic_update_index_in_dim)/dynamic_update_slice | solution.py:214
  681.1 25.6 %fusion.186 = f32[2304,8,64]{0,2,1:T(8,128)} fusion(f32[8,768,2304]{2,1,0:T(8,128)} %fusion.183, f32[8,768]{1,0:T(8,128)S(1)} %dynamic-slice_bitcast_fusion.2, pred[768,2304]{1,0:T(8,128)(4,1)S(1)} %copy.77, f32[2304,8,64]{0,2,1:T(8,128)} %get-tuple-element.688, pred[]{:T(512)S(6)} %compare.54, bf16[2304,8,64]{0,2,1:T(8,128)(2,1)} %get-tuple-element.714, ...), kind=kOutput, calls=%fused_computation.48.clone.1 | convolution fusion | flops 1870921728 | bytes 68640776 | tf_op jit(solution)/shard_map/while/body/eval_jaxpr/hqk,qhe->khe/dot_general | solution.py:208
  741.9 42.9 %multiply_reduce_fusion.2 = (f32[8,768]{1,0:T(8,128)S(1)}, f32[8,768,2304]{2,1,0:T(8,128)}) fusion(f32[8,768,2304]{2,1,0:T(8,128)} %fusion.183, f32[8,768]{1,0:T(8,128)S(1)} %dynamic-slice_bitcast_fusion.2, pred[768,2304]{1,0:T(8,128)(4,1)S(1)} %copy.77, bf16[2304,8,64]{0,2,1:T(8,128)(2,1)} %get-tuple-element.715, ...), kind=kOutput, calls=%fused_computation.38.clone.1 | convolution fusion | flops 1882712064 | bytes 118210560 | tf_op jit(solution)/shard_map/while/body/eval_jaxpr/qhe,khe->hqk/dot_general | solution.py:191
  784.8 44.8 %multiply_convert_fusion.6 = bf16[8,768,2304]{2,1,0:T(8,128)(2,1)} fusion(f32[8,768,2304]{2,1,0:T(8,128)} %get-tuple-element.614, f32[8,768,2304]{2,1,0:T(8,128)} %fusion.183, f32[8,768]{1,0:T(8,128)S(1)} %get-tuple-element.615, f32[8,768]{1,0:T(8,128)S(1)} %dynamic-slice_bitcast_fusion.2, pred[768,2304]{1,0:T(8,128)(4,1)S(1)} %copy.77), kind=kLoop, calls=%fused_computation.37.clone.1 | loop fusion | flops 84934656 | bytes 143376384 | tf_op jit(solution)/shard_map/while/body/eval_jaxpr/convert_element_type | solution.py:196
  846.3 30.3 %dynamic_update_slice.42 = f32[3,768,8,64]{1,0,3,2:T(4,128)} dynamic-update-slice(f32[3,768,8,64]{1,0,3,2:T(4,128)} %get-tuple-element.689, f32[1,768,8,64]{1,0,3,2:T(1,128)} %copy.78, s32[]{:T(128)} %get-tuple-element.686, s32[]{:T(128)} %constant.247.clone.1..sunk.1, s32[]{:T(128)} %constant.247.clone.1..sunk.1, s32[]{:T(128)} %constant.247.clone.1..sunk.1) | dynamic-update-slice | bytes 3145732 | tf_op jit(solution)/shard_map/while/body/jit(dynamic_update_index_in_dim)/dynamic_update_slice | solution.py:214
  894.5 27.0 %fusion.186 = f32[2304,8,64]{0,2,1:T(8,128)} fusion(f32[8,768,2304]{2,1,0:T(8,128)} %fusion.183, f32[8,768]{1,0:T(8,128)S(1)} %dynamic-slice_bitcast_fusion.2, pred[768,2304]{1,0:T(8,128)(4,1)S(1)} %copy.77, f32[2304,8,64]{0,2,1:T(8,128)} %get-tuple-element.688, pred[]{:T(512)S(6)} %compare.54, bf16[2304,8,64]{0,2,1:T(8,128)(2,1)} %get-tuple-element.714, ...), kind=kOutput, calls=%fused_computation.48.clone.1 | convolution fusion | flops 1870921728 | bytes 68640776 | tf_op jit(solution)/shard_map/while/body/eval_jaxpr/hqk,qhe->khe/dot_general | solution.py:208
  956.7 42.9 %multiply_reduce_fusion.2 = (f32[8,768]{1,0:T(8,128)S(1)}, f32[8,768,2304]{2,1,0:T(8,128)}) fusion(f32[8,768,2304]{2,1,0:T(8,128)} %fusion.183, f32[8,768]{1,0:T(8,128)S(1)} %dynamic-slice_bitcast_fusion.2, pred[768,2304]{1,0:T(8,128)(4,1)S(1)} %copy.77, bf16[2304,8,64]{0,2,1:T(8,128)(2,1)} %get-tuple-element.715, ...), kind=kOutput, calls=%fused_computation.38.clone.1 | convolution fusion | flops 1882712064 | bytes 118210560 | tf_op jit(solution)/shard_map/while/body/eval_jaxpr/qhe,khe->hqk/dot_general | solution.py:191
  999.6 44.8 %multiply_convert_fusion.6 = bf16[8,768,2304]{2,1,0:T(8,128)(2,1)} fusion(f32[8,768,2304]{2,1,0:T(8,128)} %get-tuple-element.614, f32[8,768,2304]{2,1,0:T(8,128)} %fusion.183, f32[8,768]{1,0:T(8,128)S(1)} %get-tuple-element.615, f32[8,768]{1,0:T(8,128)S(1)} %dynamic-slice_bitcast_fusion.2, pred[768,2304]{1,0:T(8,128)(4,1)S(1)} %copy.77), kind=kLoop, calls=%fused_computation.37.clone.1 | loop fusion | flops 84934656 | bytes 143376384 | tf_op jit(solution)/shard_map/while/body/eval_jaxpr/convert_element_type | solution.py:196
  1061.1 30.3 %dynamic_update_slice.42 = f32[3,768,8,64]{1,0,3,2:T(4,128)} dynamic-update-slice(f32[3,768,8,64]{1,0,3,2:T(4,128)} %get-tuple-element.689, f32[1,768,8,64]{1,0,3,2:T(1,128)} %copy.78, s32[]{:T(128)} %get-tuple-element.686, s32[]{:T(128)} %constant.247.clone.1..sunk.1, s32[]{:T(128)} %constant.247.clone.1..sunk.1, s32[]{:T(128)} %constant.247.clone.1..sunk.1) | dynamic-update-slice | bytes 3145732 | tf_op jit(solution)/shard_map/while/body/jit(dynamic_update_index_in_dim)/dynamic_update_slice | solution.py:214
  1109.3 27.0 %fusion.186 = f32[2304,8,64]{0,2,1:T(8,128)} fusion(f32[8,768,2304]{2,1,0:T(8,128)} %fusion.183, f32[8,768]{1,0:T(8,128)S(1)} %dynamic-slice_bitcast_fusion.2, pred[768,2304]{1,0:T(8,128)(4,1)S(1)} %copy.77, f32[2304,8,64]{0,2,1:T(8,128)} %get-tuple-element.688, pred[]{:T(512)S(6)} %compare.54, bf16[2304,8,64]{0,2,1:T(8,128)(2,1)} %get-tuple-element.714, ...), kind=kOutput, calls=%fused_computation.48.clone.1 | convolution fusion | flops 1870921728 | bytes 68640776 | tf_op jit(solution)/shard_map/while/body/eval_jaxpr/hqk,qhe->khe/dot_general | solution.py:208
  1185.1 26.4 %fusion.123 = f32[2304,2048]{1,0:T(8,128)} fusion(bf16[2304,2048]{1,0:T(8,128)(2,1)} %all-gather.7.cloned.1.call-done, bf16[2048,2048]{1,0:T(8,128)(2,1)} %all-gather.13.cloned.1.call-done), kind=kOutput, calls=%fused_computation.256 | convolution fusion | flops 19327352832 | bytes 36700160 | tf_op jit(solution)/shard_map/dot_general | solution.py:151
  1211.5 39.5 %convert_reduce_fusion = (f32[2048]{0:T(1024)}, bf16[2304,2048]{1,0:T(8,128)(2,1)}) fusion(f32[2304,2048]{1,0:T(8,128)} %fusion.123, f32[2048]{0:T(1024)S(1)} %copy-done.25, bf16[2304,2048]{1,0:T(8,128)(2,1)} %all-gather.17.cloned.1.call-done, bf16[2048,2048]{1,0:T(8,128)(2,1)} %all-gather.15.cloned.1.call-done), kind=kOutput, calls=%fused_computation.94 | convolution fusion | flops 19435878400 | bytes 46153728 | tf_op jit(solution)/shard_map/td,fd->tf/dot_general | solution.py:170
  1251.1 28.0 %fusion.59 = bf16[2304,2048]{1,0:T(8,128)(2,1)} fusion(f32[2304,2048,1]{1,0,2:T(8,128)} %fusion.119, bf16[2304,2048]{1,0:T(8,128)(2,1)} %get-tuple-element.444, bf16[2048,2048]{1,0:T(8,128)(2,1)} %all-gather.13.cloned.1.call-done), kind=kOutput, calls=%fused_computation.93 | convolution fusion | flops 19336790016 | bytes 46137344 | tf_op jit(solution)/shard_map/tf,df->td/dot_general | solution.py:246
  1294.2 32.4 %convolution_add_fusion = f32[2304,2048]{1,0:T(8,128)} fusion(f32[2304,2048]{1,0:T(8,128)} %fusion.122, bf16[2048,2048]{1,0:T(8,128)(2,1)} %all-gather.15.cloned.1.call-done, f32[2304,2048]{1,0:T(8,128)} %fusion.123, f32[2048]{0:T(1024)S(1)} %copy-done.25), kind=kOutput, calls=%fused_computation.98 | convolution fusion | flops 19379257344 | bytes 65019904 | tf_op jit(solution)/shard_map/dot_general | solution.py:155
  1358.0 26.6 %convolution_convert_fusion.1 = bf16[2048,2048]{1,0:T(8,128)(2,1)} fusion(bf16[2304,2048]{1,0:T(8,128)(2,1)} %all-gather.7.cloned.1.call-done, bf16[2304,2048]{1,0:T(8,128)(2,1)} %get-tuple-element.444), kind=kOutput, calls=%fused_computation.104 | convolution fusion | flops 19331547136 | bytes 27262976 | tf_op jit(solution)/shard_map/td,tf->df/dot_general | solution.py:174
  1384.7 31.1 %convolution_convert_fusion = bf16[2048,2048]{1,0:T(8,128)(2,1)} fusion(bf16[2304,2048]{1,0:T(8,128)(2,1)} %all-gather.17.cloned.1.call-done, f32[2304,2048]{1,0:T(8,128)} %fusion.123, f32[2048]{0:T(1024)S(1)} %copy-done.25), kind=kOutput, calls=%fused_computation.103 | convolution fusion | flops 19378733056 | bytes 36708352 | tf_op jit(solution)/shard_map/tf,td->fd/dot_general | solution.py:173
  1437.2 30.7 %all-reduce.6.cloned.1.call-done = bf16[2304,2048]{1,0:T(8,128)(2,1)} async-done(((bf16[2304,2048]{1,0:T(8,128)(2,1)}), bf16[2304,2048]{1,0:T(8,128)(2,1)}) %all-reduce.6.cloned.1.call-update) | async-done | bytes 9437200 | tf_op jit(solution)/shard_map/psum | solution.py:243
  1474.5 338.8 %all-reduce.4.cloned.1.call-done = f32[2304,2048]{1,0:T(8,128)} async-done(((f32[2304,2048]{1,0:T(8,128)}), f32[2304,2048]{1,0:T(8,128)}) %all-reduce.4.cloned.1.call-update) | async-done | bytes 18874384 | tf_op jit(solution)/shard_map/psum | solution.py:153
  1823.4 29.3 %all-reduce = (f32[3,512]{1,0:T(4,128)}, f32[2048]{0:T(1024)}) all-reduce(f32[3,512]{1,0:T(4,128)S(1)} %convert_reduce_fusion.1, f32[2048]{0:T(1024)S(1)} %copy-done.21), channel_id=1, replica_groups=mesh['dp'=8,'tensor'=4] {'dp'}, use_global_device_ids=true, to_apply=%region_38.39 | all-reduce | flops 3584 | bytes 28672 | tf_op jit(solution)/shard_map/psum | solution.py:242
  1855.2 69.3 %reduce-scatter.8.cloned.1.call-done = bf16[3,256,512]{1,2,0:T(8,128)(2,1)} async-done(((bf16[3,2048,512]{1,2,0:T(8,128)(2,1)}), bf16[3,256,512]{1,2,0:T(8,128)(2,1)}) %reduce-scatter.8.cloned.1.call-update) | async-done | bytes 786448 | tf_op jit(solution)/shard_map/reduce_scatter | solution.py:229
  1927.0 87.8 %reduce-scatter.12.cloned.1.call-done = bf16[256,2048]{1,0:T(8,128)(2,1)} async-done(((bf16[2048,2048]{1,0:T(8,128)(2,1)}), bf16[256,2048]{1,0:T(8,128)(2,1)}) %reduce-scatter.12.cloned.1.call-update) | async-done | bytes 1048592 | tf_op jit(solution)/shard_map/reduce_scatter | solution.py:235
  2017.6 87.4 %reduce-scatter.14.cloned.1.call-done = bf16[2048,256]{1,0:T(8,128)(2,1)} async-done(((bf16[2048,2048]{1,0:T(8,128)(2,1)}), bf16[2048,256]{1,0:T(8,128)(2,1)}) %reduce-scatter.14.cloned.1.call-update) | async-done | bytes 1048592 | tf_op jit(solution)/shard_map/reduce_scatter | solution.py:238
  2107.8 133.0 %reduce-scatter.16.cloned.1.call-done = f32[64,3]{1,0:T(8,128)} async-done(((f32[2048,3]{1,0:T(8,128)}), f32[64,3]{1,0:T(8,128)}) %reduce-scatter.16.cloned.1.call-update) | async-done | bytes 784
  (245 shorter events, 562.1 us)
Async XLA Ops:
  7.2 4.7 copy-start.1
  7.2 6.6 copy-start.13
  7.2 6.6 copy-start.20
  7.2 70.9 %all-gather.9.cloned.1.call-start = ((), (), s32[]{:S(2)}) async-start(), calls=%async_computation.6 | async-start | bytes 7077888 | tf_op jit(solution)/shard_map/all_gather | solution.py:117
  9.7 164.8 %all-gather.7.cloned.1.call-start = ((), (), s32[]{:S(2)}) async-start(), calls=%async_computation.5 | async-start | bytes 11796480 | tf_op jit(solution)/shard_map/all_gather | solution.py:122
  16.2 158.4 %copy-start.24 = (f32[3,512]{1,0:T(4,128)S(1)}, f32[3,512]{1,0:T(4,128)}, u32[]{:S(2)}) copy-start(f32[3,512]{1,0:T(4,128)} %param.21) | copy-start | bytes 18436
  16.2 452.5 %all-gather.11.cloned.1.call-start = ((), (), s32[]{:S(2)}) async-start(), calls=%async_computation.7 | async-start | bytes 2359296 | tf_op jit(solution)/shard_map/all_gather | solution.py:118
  16.9 451.8 %all-gather.17.cloned.1.call-start = ((), (), s32[]{:S(2)}) async-start(), calls=%async_computation.11 | async-start | bytes 11796480 | tf_op jit(solution)/shard_map/all_gather | solution.py:165
  17.5 1167.6 %all-gather.13.cloned.1.call-start = ((), (), s32[]{:S(2)}) async-start(), calls=%async_computation.8 | async-start | bytes 9437184 | tf_op jit(solution)/shard_map/all_gather | solution.py:119
  18.1 1193.4 %all-gather.15.cloned.1.call-start = ((), (), s32[]{:S(2)}) async-start(), calls=%async_computation.9 | async-start | bytes 9437184 | tf_op jit(solution)/shard_map/all_gather | solution.py:120
  18.7 1449.3 %all-reduce.6.cloned.1.call-start = ((), (), s32[]{:S(2)}) async-start(), calls=%async_computation.12 | async-start | bytes 18874368 | tf_op jit(solution)/shard_map/psum | solution.py:243
  21.2 183.4 %copy-start.7 = (f32[2304,16]{0,1:T(8,128)}, f32[2304,16]{0,1:T(8,128)S(1)}, u32[]{:S(2)}) copy-start(f32[2304,16]{0,1:T(8,128)S(1)} %get-tuple-element.470) | copy-start | bytes 442372
  21.2 183.3 %copy-start.9 = (f32[2304,16]{0,1:T(8,128)}, f32[2304,16]{0,1:T(8,128)S(1)}, u32[]{:S(2)}) copy-start(f32[2304,16]{0,1:T(8,128)S(1)} %get-tuple-element.471) | copy-start | bytes 442372
  1136.6 12.4 copy-start.8
  1136.6 12.4 copy-start.10
  1145.1 3.9 copy-start
  1185.1 26.4 %copy-start.25 = (f32[2048]{0:T(1024)S(1)}, f32[2048]{0:T(1024)}, u32[]{:S(2)}) copy-start(f32[2048]{0:T(1024)} %param.24) | copy-start | bytes 24580
  1279.1 534.1 %all-reduce.4.cloned.1.call-start = ((), (), s32[]{:S(2)}) async-start(), calls=%async_computation.10 | async-start | bytes 37748736 | tf_op jit(solution)/shard_map/psum | solution.py:153
  1326.6 9.6 copy-start.3
  1326.7 526.7 %reduce-scatter.10.cloned.1.call-start = ((), (), s32[]{:S(2)}) async-start(), calls=%async_computation.14 | async-start | bytes 2359296 | tf_op jit(solution)/shard_map/reduce_scatter | solution.py:232
  1336.2 588.3 %reduce-scatter.8.cloned.1.call-start = ((), (), s32[]{:S(2)}) async-start(), calls=%async_computation.13 | async-start | bytes 7077888 | tf_op jit(solution)/shard_map/reduce_scatter | solution.py:229
  1357.9 656.9 %reduce-scatter.12.cloned.1.call-start = ((), (), s32[]{:S(2)}) async-start(), calls=%async_computation.15 | async-start | bytes 9437184 | tf_op jit(solution)/shard_map/reduce_scatter | solution.py:235
  1384.6 720.5 %reduce-scatter.14.cloned.1.call-start = ((), (), s32[]{:S(2)}) async-start(), calls=%async_computation.16 | async-start | bytes 9437184 | tf_op jit(solution)/shard_map/reduce_scatter | solution.py:238
  1415.8 52.2 %copy-start.2 = (bf16[576,2048]{1,0:T(8,128)(2,1)S(1)}, bf16[576,2048]{1,0:T(8,128)(2,1)}, u32[]{:S(2)}) copy-start(bf16[576,2048]{1,0:T(8,128)(2,1)} %param.16) | copy-start | bytes 7077892
  1415.8 52.2 %copy-start.12 = (f32[576]{0:T(1024)S(1)}, f32[576]{0:T(1024)}, u32[]{:S(2)}) copy-start(f32[576]{0:T(1024)} %copy-done.11) | copy-start | bytes 6916
  1415.8 52.2 %copy-start.14 = (f32[2048]{0:T(1024)S(1)}, f32[2048]{0:T(1024)}, u32[]{:S(2)}) copy-start(f32[2048]{0:T(1024)} %param.18) | copy-start | bytes 24580
  1415.8 824.9 %reduce-scatter.16.cloned.1.call-start = ((), (), s32[]{:S(2)}) async-start(), calls=%async_computation.17 | async-start | bytes 1081344
  1433.1 37.6 %copy-start.18 = (f32[576]{0:T(1024)S(1)}, f32[576]{0:T(1024)}, u32[]{:S(2)}) copy-start(f32[576]{0:T(1024)} %copy-done.17) | copy-start | bytes 6916
  1433.1 37.6 %copy-start.16 = (f32[576]{0:T(1024)S(1)}, f32[576]{0:T(1024)}, u32[]{:S(2)}) copy-start(f32[576]{0:T(1024)} %copy-done.15) | copy-start | bytes 6916
  1437.2 376.1 %copy-start.19 = (f32[2048]{0:T(1024)S(1)}, f32[2048]{0:T(1024)}, u32[]{:S(2)}) copy-start(f32[2048]{0:T(1024)} %param.26) | copy-start | bytes 24580
  1474.5 348.0 %copy-start.6 = (bf16[3,256,512]{2,1,0:T(8,128)(2,1)S(1)}, bf16[3,256,512]{2,1,0:T(8,128)(2,1)}, u32[]{:S(2)}) copy-start(bf16[3,256,512]{2,1,0:T(8,128)(2,1)} %param.20) | copy-start | bytes 2359300
  1474.5 348.9 %copy-start.21 = (f32[2048]{0:T(1024)S(1)}, f32[2048]{0:T(1024)}, u32[]{:S(2)}) copy-start(f32[2048]{0:T(1024)} %get-tuple-element.443) | copy-start | bytes 24580
  (8 other events, 12.8 us)
Sparse Core Ops, SparseCore 0:
  10.2 67.8 all-gather.8
  80.0 94.5 all-gather.6
  176.2 30.8 all-gather.10
  208.7 95.3 all-gather.16
  305.6 82.0 all-gather.12
  389.1 81.0 all-gather.14
  1279.2 188.6 all-reduce.5
  1471.5 341.7 all-reduce.3
  1816.2 37.0 reduce-scatter.9
  1855.6 68.7 reduce-scatter.7
  1926.9 87.9 reduce-scatter.11
  2017.1 87.9 reduce-scatter.13
  2107.4 133.2 reduce-scatter.15
where the time goes:
time: 2260 us; the launch traced here: 2250 us
  waiting for transfers between devices  903 us (40%)
  matrix products  798 us (35%)
  other arithmetic  263 us (12%)
  local copies, waits for them, and re-layouts  174 us (8%)
  loops' own time  50.7 us (2%)
  blocking collectives  45.8 us (2%)
    psum x1, waiting for transfers between devices, body(): lax.psum(jnp.dot(attended, out_w, preferred_element_type=jnp.float32) + j...  339 us
    unnamed x14, waiting for transfers between devices  135 us
    convert_element_type x3, other arithmetic, back_block(): grad_scores = (probs_f * (grad_probs - jnp.sum(probs_f * grad_probs, axis...  134 us
    dot_general x3, matrix products, back_block(): jnp.einsum('qhe,khe->hqk', grad_rows, values_all, preferred_element_type=...  129 us
    dynamic_update_slice x6, local copies, waits for them, and re-layouts, body(): lax.scan(back_block, (zero_heads, zero_heads), (block_starts, log_totals))  99.3 us
    all_gather x1, waiting for transfers between devices, body(): normed = lax.all_gather(normed_local, 'tensor', axis=0, tiled=True)  96.4 us
    reduce_scatter x1, waiting for transfers between devices, body(): lax.psum_scatter(grad_w_fc1.astype(jnp.bfloat16), 'dp', scatter_dimension...  87.8 us
    reduce_scatter x1, waiting for transfers between devices, body(): lax.psum_scatter(grad_w_fc2.astype(jnp.bfloat16), 'dp', scatter_dimension...  87.4 us
  transfers between devices with their start and end apart: 13, of which 9 were waited for; matrix products, arithmetic and copies ran while one was open for 51% of the time, Pallas kernels for 0%

commit v1 on v0

--- a/solution.py
+++ b/solution.py
@@ -150,10 +150,13 @@
     attended = attended.reshape(total_rows, head_count * HDIM)
     hidden_pre = jnp.dot(normed, up_w, preferred_element_type=jnp.float32) + b_fc1
     activated = gelu_tanh(hidden_pre).astype(jnp.bfloat16)
-    branch_whole = lax.psum(
-        jnp.dot(attended, out_w, preferred_element_type=jnp.float32)
-        + jnp.dot(activated, down_w, preferred_element_type=jnp.float32),
-        "tensor",
+    branch_whole = jnp.sum(
+        lax.all_gather(
+            jnp.dot(attended, out_w, preferred_element_type=jnp.float32)
+            + jnp.dot(activated, down_w, preferred_element_type=jnp.float32),
+            "tensor",
+        ),
+        axis=0,
     )
     branch_sum = lax.dynamic_slice_in_dim(branch_whole, own_start, local_rows, 0)
     output_rows = (tokens_f + branch_sum + resid_bias).astype(jnp.bfloat16)

time: 2260 us -> 2560 us (1.13)
  waiting for transfers between devices: 903 us -> 1170 us
  other arithmetic: 263 us -> 294 us
    all_gather x0 -> x1, waiting for transfers between devices: none -> 642 us  [body(): lax.all_gather(jnp.dot(attended, out_w, preferred_element_type=jnp.float3...]
    psum x1 -> x0, waiting for transfers between devices: 339 us -> none  [body(): lax.psum(jnp.dot(attended, out_w, preferred_element_type=jnp.float32) + j...]
    reduce_scatter x1, waiting for transfers between devices: 69.3 us -> 36.2 us  [body(): lax.psum_scatter(grad_w_qkv.astype(jnp.bfloat16), 'dp', scatter_dimension...]
    reduce_sum x0 -> x1, other arithmetic: none -> 31.3 us  [body(): jnp.sum(lax.all_gather(jnp.dot(attended, out_w, preferred_element_type=jn...]
  transfers between devices with their start and end apart: 13 -> 13, of which waited for: 9 -> 8; matrix products, arithmetic and copies ran while one was open for 51% -> 47% of each run, Pallas kernels for 0% -> 0%
where the time goes in v1:
time: 2560 us; the launch traced here: 2550 us
  waiting for transfers between devices  1170 us (46%)
  matrix products  798 us (31%)
  other arithmetic  294 us (11%)
  local copies, waits for them, and re-layouts  173 us (7%)
  loops' own time  50.7 us (2%)
  blocking collectives  47.1 us (2%)
    all_gather x1, waiting for transfers between devices, body(): lax.all_gather(jnp.dot(attended, out_w, preferred_element_type=jnp.float3...  642 us
    unnamed x14, waiting for transfers between devices  135 us
    convert_element_type x3, other arithmetic, back_block(): grad_scores = (probs_f * (grad_probs - jnp.sum(probs_f * grad_probs, axis...  134 us
    dot_general x3, matrix products, back_block(): jnp.einsum('qhe,khe->hqk', grad_rows, values_all, preferred_element_type=...  129 us
    dynamic_update_slice x6, local copies, waits for them, and re-layouts, body(): lax.scan(back_block, (zero_heads, zero_heads), (block_starts, log_totals))  99.3 us
    all_gather x1, waiting for transfers between devices, body(): normed = lax.all_gather(normed_local, 'tensor', axis=0, tiled=True)  96.4 us
    reduce_scatter x1, waiting for transfers between devices, body(): lax.psum_scatter(grad_w_fc1.astype(jnp.bfloat16), 'dp', scatter_dimension...  87.7 us
    reduce_scatter x1, waiting for transfers between devices, body(): lax.psum_scatter(grad_w_fc2.astype(jnp.bfloat16), 'dp', scatter_dimension...  87.3 us
  transfers between devices with their start and end apart: 13, of which 8 were waited for; matrix products, arithmetic and copies ran while one was open for 47% of the time, Pallas kernels for 0%

profile of v1, /device:TPU:0, one launch (start us, length us, event | category | flops | bytes accessed | tf_op | source)
XLA Modules:
  0.0 2550.8 jit_solution(13124576986834934755)
XLA Ops:
  21.2 56.9 %all-gather.11.cloned.1.call-done = bf16[3,2048,512]{1,2,0:T(8,128)(2,1)} async-done(((bf16[3,256,512]{1,2,0:T(8,128)(2,1)}), bf16[3,2048,512]{1,2,0:T(8,128)(2,1)}) %all-gather.11.cloned.1.call-update) | async-done | bytes 6291472 | tf_op jit(solution)/shard_map/all_gather | solution.py:117
  78.1 96.4 %all-gather.9.cloned.1.call-done = bf16[2304,2048]{1,0:T(8,128)(2,1)} async-done(((bf16[576,2048]{1,0:T(8,128)(2,1)}), bf16[2304,2048]{1,0:T(8,128)(2,1)}) %all-gather.9.cloned.1.call-update) | async-done | bytes 9437200 | tf_op jit(solution)/shard_map/all_gather | solution.py:122
  207.6 261.1 %while.35 = (s32[]{:T(128)}, bf16[3,768,8,64]{1,3,2,0:T(8,128)(2,1)}, f32[3,8,768]{2,1,0:T(8,128)}, f32[3,8]{1,0:T(4,128)}, s32[3]{0:T(128)S(1)}, /*index=5*/pre...) while((s32[]{:T(128)}, ...), condition=%wide.region_24.25_spmd, body=%wide.region_20.24_spmd.sunk | while | flops 3817168896 | bytes 187103536 | solution.py:149
  229.5 25.1 fusion.171
  442.8 24.6 fusion.173
  479.2 657.4 %while.36 = (s32[]{:T(128)}, f32[2304,8,64]{0,2,1:T(8,128)}, f32[2304,8,64]{0,2,1:T(8,128)}, f32[3,768,8,64]{1,0,3,2:T(4,128)}, s32[3]{0:T(128)S(1)}, /*index=5*...) while((s32[]{:T(128)}, f32[2304,8,64]{0,2,1:T(8,128)}, ...), condition=%wide.region_28.29_spmd.clone, body=%wide.region_26.28_spmd.clone.sunk | while | flops 9287196672 | bytes 472552672 | solution.py:217
  529.8 42.9 %multiply_reduce_fusion.2 = (f32[8,768]{1,0:T(8,128)S(1)}, f32[8,768,2304]{2,1,0:T(8,128)}) fusion(f32[8,768,2304]{2,1,0:T(8,128)} %fusion.183, f32[8,768]{1,0:T(8,128)S(1)} %dynamic-slice_bitcast_fusion.2, pred[768,2304]{1,0:T(8,128)(4,1)S(1)} %copy.78, bf16[2304,8,64]{0,2,1:T(8,128)(2,1)} %get-tuple-element.715, ...), kind=kOutput, calls=%fused_computation.38.clone.1 | convolution fusion | flops 1882712064 | bytes 118210560 | tf_op jit(solution)/shard_map/while/body/eval_jaxpr/qhe,khe->hqk/dot_general | solution.py:194
  572.7 44.8 %multiply_convert_fusion.6 = bf16[8,768,2304]{2,1,0:T(8,128)(2,1)} fusion(f32[8,768,2304]{2,1,0:T(8,128)} %get-tuple-element.614, f32[8,768,2304]{2,1,0:T(8,128)} %fusion.183, f32[8,768]{1,0:T(8,128)S(1)} %get-tuple-element.615, f32[8,768]{1,0:T(8,128)S(1)} %dynamic-slice_bitcast_fusion.2, pred[768,2304]{1,0:T(8,128)(4,1)S(1)} %copy.78), kind=kLoop, calls=%fused_computation.37.clone.1 | loop fusion | flops 84934656 | bytes 143376384 | tf_op jit(solution)/shard_map/while/body/eval_jaxpr/convert_element_type | solution.py:199
  634.2 30.3 %dynamic_update_slice.42 = f32[3,768,8,64]{1,0,3,2:T(4,128)} dynamic-update-slice(f32[3,768,8,64]{1,0,3,2:T(4,128)} %get-tuple-element.689, f32[1,768,8,64]{1,0,3,2:T(1,128)} %copy.79, s32[]{:T(128)} %get-tuple-element.686, s32[]{:T(128)} %constant.247.clone.1..sunk.1, s32[]{:T(128)} %constant.247.clone.1..sunk.1, s32[]{:T(128)} %constant.247.clone.1..sunk.1) | dynamic-update-slice | bytes 3145732 | tf_op jit(solution)/shard_map/while/body/jit(dynamic_update_index_in_dim)/dynamic_update_slice | solution.py:217
  681.1 25.6 %fusion.186 = f32[2304,8,64]{0,2,1:T(8,128)} fusion(f32[8,768,2304]{2,1,0:T(8,128)} %fusion.183, f32[8,768]{1,0:T(8,128)S(1)} %dynamic-slice_bitcast_fusion.2, pred[768,2304]{1,0:T(8,128)(4,1)S(1)} %copy.78, f32[2304,8,64]{0,2,1:T(8,128)} %get-tuple-element.688, pred[]{:T(512)S(6)} %compare.54, bf16[2304,8,64]{0,2,1:T(8,128)(2,1)} %get-tuple-element.714, ...), kind=kOutput, calls=%fused_computation.48.clone.1 | convolution fusion | flops 1870921728 | bytes 68640776 | tf_op jit(solution)/shard_map/while/body/eval_jaxpr/hqk,qhe->khe/dot_general | solution.py:211
  741.9 42.9 %multiply_reduce_fusion.2 = (f32[8,768]{1,0:T(8,128)S(1)}, f32[8,768,2304]{2,1,0:T(8,128)}) fusion(f32[8,768,2304]{2,1,0:T(8,128)} %fusion.183, f32[8,768]{1,0:T(8,128)S(1)} %dynamic-slice_bitcast_fusion.2, pred[768,2304]{1,0:T(8,128)(4,1)S(1)} %copy.78, bf16[2304,8,64]{0,2,1:T(8,128)(2,1)} %get-tuple-element.715, ...), kind=kOutput, calls=%fused_computation.38.clone.1 | convolution fusion | flops 1882712064 | bytes 118210560 | tf_op jit(solution)/shard_map/while/body/eval_jaxpr/qhe,khe->hqk/dot_general | solution.py:194
  784.8 44.8 %multiply_convert_fusion.6 = bf16[8,768,2304]{2,1,0:T(8,128)(2,1)} fusion(f32[8,768,2304]{2,1,0:T(8,128)} %get-tuple-element.614, f32[8,768,2304]{2,1,0:T(8,128)} %fusion.183, f32[8,768]{1,0:T(8,128)S(1)} %get-tuple-element.615, f32[8,768]{1,0:T(8,128)S(1)} %dynamic-slice_bitcast_fusion.2, pred[768,2304]{1,0:T(8,128)(4,1)S(1)} %copy.78), kind=kLoop, calls=%fused_computation.37.clone.1 | loop fusion | flops 84934656 | bytes 143376384 | tf_op jit(solution)/shard_map/while/body/eval_jaxpr/convert_element_type | solution.py:199
  846.3 30.3 %dynamic_update_slice.42 = f32[3,768,8,64]{1,0,3,2:T(4,128)} dynamic-update-slice(f32[3,768,8,64]{1,0,3,2:T(4,128)} %get-tuple-element.689, f32[1,768,8,64]{1,0,3,2:T(1,128)} %copy.79, s32[]{:T(128)} %get-tuple-element.686, s32[]{:T(128)} %constant.247.clone.1..sunk.1, s32[]{:T(128)} %constant.247.clone.1..sunk.1, s32[]{:T(128)} %constant.247.clone.1..sunk.1) | dynamic-update-slice | bytes 3145732 | tf_op jit(solution)/shard_map/while/body/jit(dynamic_update_index_in_dim)/dynamic_update_slice | solution.py:217
  894.5 27.0 %fusion.186 = f32[2304,8,64]{0,2,1:T(8,128)} fusion(f32[8,768,2304]{2,1,0:T(8,128)} %fusion.183, f32[8,768]{1,0:T(8,128)S(1)} %dynamic-slice_bitcast_fusion.2, pred[768,2304]{1,0:T(8,128)(4,1)S(1)} %copy.78, f32[2304,8,64]{0,2,1:T(8,128)} %get-tuple-element.688, pred[]{:T(512)S(6)} %compare.54, bf16[2304,8,64]{0,2,1:T(8,128)(2,1)} %get-tuple-element.714, ...), kind=kOutput, calls=%fused_computation.48.clone.1 | convolution fusion | flops 1870921728 | bytes 68640776 | tf_op jit(solution)/shard_map/while/body/eval_jaxpr/hqk,qhe->khe/dot_general | solution.py:211
  956.7 42.9 %multiply_reduce_fusion.2 = (f32[8,768]{1,0:T(8,128)S(1)}, f32[8,768,2304]{2,1,0:T(8,128)}) fusion(f32[8,768,2304]{2,1,0:T(8,128)} %fusion.183, f32[8,768]{1,0:T(8,128)S(1)} %dynamic-slice_bitcast_fusion.2, pred[768,2304]{1,0:T(8,128)(4,1)S(1)} %copy.78, bf16[2304,8,64]{0,2,1:T(8,128)(2,1)} %get-tuple-element.715, ...), kind=kOutput, calls=%fused_computation.38.clone.1 | convolution fusion | flops 1882712064 | bytes 118210560 | tf_op jit(solution)/shard_map/while/body/eval_jaxpr/qhe,khe->hqk/dot_general | solution.py:194
  999.6 44.8 %multiply_convert_fusion.6 = bf16[8,768,2304]{2,1,0:T(8,128)(2,1)} fusion(f32[8,768,2304]{2,1,0:T(8,128)} %get-tuple-element.614, f32[8,768,2304]{2,1,0:T(8,128)} %fusion.183, f32[8,768]{1,0:T(8,128)S(1)} %get-tuple-element.615, f32[8,768]{1,0:T(8,128)S(1)} %dynamic-slice_bitcast_fusion.2, pred[768,2304]{1,0:T(8,128)(4,1)S(1)} %copy.78), kind=kLoop, calls=%fused_computation.37.clone.1 | loop fusion | flops 84934656 | bytes 143376384 | tf_op jit(solution)/shard_map/while/body/eval_jaxpr/convert_element_type | solution.py:199
  1061.0 30.3 %dynamic_update_slice.42 = f32[3,768,8,64]{1,0,3,2:T(4,128)} dynamic-update-slice(f32[3,768,8,64]{1,0,3,2:T(4,128)} %get-tuple-element.689, f32[1,768,8,64]{1,0,3,2:T(1,128)} %copy.79, s32[]{:T(128)} %get-tuple-element.686, s32[]{:T(128)} %constant.247.clone.1..sunk.1, s32[]{:T(128)} %constant.247.clone.1..sunk.1, s32[]{:T(128)} %constant.247.clone.1..sunk.1) | dynamic-update-slice | bytes 3145732 | tf_op jit(solution)/shard_map/while/body/jit(dynamic_update_index_in_dim)/dynamic_update_slice | solution.py:217
  1109.2 27.0 %fusion.186 = f32[2304,8,64]{0,2,1:T(8,128)} fusion(f32[8,768,2304]{2,1,0:T(8,128)} %fusion.183, f32[8,768]{1,0:T(8,128)S(1)} %dynamic-slice_bitcast_fusion.2, pred[768,2304]{1,0:T(8,128)(4,1)S(1)} %copy.78, f32[2304,8,64]{0,2,1:T(8,128)} %get-tuple-element.688, pred[]{:T(512)S(6)} %compare.54, bf16[2304,8,64]{0,2,1:T(8,128)(2,1)} %get-tuple-element.714, ...), kind=kOutput, calls=%fused_computation.48.clone.1 | convolution fusion | flops 1870921728 | bytes 68640776 | tf_op jit(solution)/shard_map/while/body/eval_jaxpr/hqk,qhe->khe/dot_general | solution.py:211
  1185.0 26.4 %fusion.123 = f32[2304,2048]{1,0:T(8,128)} fusion(bf16[2304,2048]{1,0:T(8,128)(2,1)} %all-gather.9.cloned.1.call-done, bf16[2048,2048]{1,0:T(8,128)(2,1)} %all-gather.15.cloned.1.call-done), kind=kOutput, calls=%fused_computation.256 | convolution fusion | flops 19327352832 | bytes 36700160 | tf_op jit(solution)/shard_map/dot_general | solution.py:151
  1211.5 39.5 %convert_reduce_fusion = (f32[2048]{0:T(1024)}, bf16[2304,2048]{1,0:T(8,128)(2,1)}) fusion(f32[2304,2048]{1,0:T(8,128)} %fusion.123, f32[2048]{0:T(1024)S(1)} %copy-done.25, bf16[2304,2048]{1,0:T(8,128)(2,1)} %all-gather.19.cloned.1.call-done, bf16[2048,2048]{1,0:T(8,128)(2,1)} %all-gather.17.cloned.1.call-done), kind=kOutput, calls=%fused_computation.94 | convolution fusion | flops 19435878400 | bytes 46153728 | tf_op jit(solution)/shard_map/td,fd->tf/dot_general | solution.py:173
  1251.0 28.2 %fusion.59 = bf16[2304,2048]{1,0:T(8,128)(2,1)} fusion(f32[2304,2048,1]{1,0,2:T(8,128)} %fusion.119, bf16[2304,2048]{1,0:T(8,128)(2,1)} %get-tuple-element.444, bf16[2048,2048]{1,0:T(8,128)(2,1)} %all-gather.15.cloned.1.call-done), kind=kOutput, calls=%fused_computation.93 | convolution fusion | flops 19336790016 | bytes 46137344 | tf_op jit(solution)/shard_map/tf,df->td/dot_general | solution.py:249
  1294.4 32.4 %convolution_add_fusion = f32[2304,2048]{1,0:T(8,128)} fusion(f32[2304,2048]{1,0:T(8,128)} %fusion.122, bf16[2048,2048]{1,0:T(8,128)(2,1)} %all-gather.17.cloned.1.call-done, f32[2304,2048]{1,0:T(8,128)} %fusion.123, f32[2048]{0:T(1024)S(1)} %copy-done.25), kind=kOutput, calls=%fused_computation.98 | convolution fusion | flops 19379257344 | bytes 65019904 | tf_op jit(solution)/shard_map/dot_general | solution.py:156
  1358.1 26.6 %convolution_convert_fusion.1 = bf16[2048,2048]{1,0:T(8,128)(2,1)} fusion(bf16[2304,2048]{1,0:T(8,128)(2,1)} %all-gather.9.cloned.1.call-done, bf16[2304,2048]{1,0:T(8,128)(2,1)} %get-tuple-element.444), kind=kOutput, calls=%fused_computation.104 | convolution fusion | flops 19331547136 | bytes 27262976 | tf_op jit(solution)/shard_map/td,tf->df/dot_general | solution.py:177
  1384.8 31.1 %convolution_convert_fusion = bf16[2048,2048]{1,0:T(8,128)(2,1)} fusion(bf16[2304,2048]{1,0:T(8,128)(2,1)} %all-gather.19.cloned.1.call-done, f32[2304,2048]{1,0:T(8,128)} %fusion.123, f32[2048]{0:T(1024)S(1)} %copy-done.25), kind=kOutput, calls=%fused_computation.103 | convolution fusion | flops 19378733056 | bytes 36708352 | tf_op jit(solution)/shard_map/tf,td->fd/dot_general | solution.py:176
  1437.6 30.4 %all-reduce.3.cloned.1.call-done = bf16[2304,2048]{1,0:T(8,128)(2,1)} async-done(((bf16[2304,2048]{1,0:T(8,128)(2,1)}), bf16[2304,2048]{1,0:T(8,128)(2,1)}) %all-reduce.3.cloned.1.call-update) | async-done | bytes 9437200 | tf_op jit(solution)/shard_map/psum | solution.py:246
  1474.5 642.5 %all-gather.21.cloned.1.call-done = f32[9216,2048]{1,0:T(8,128)} async-done(((f32[2304,2048]{1,0:T(8,128)}), f32[9216,2048]{1,0:T(8,128)}) %all-gather.21.cloned.1.call-update) | async-done | bytes 75497488 | tf_op jit(solution)/shard_map/all_gather | solution.py:154
  2117.0 31.3 %reduce_sum.322 = f32[2304,2048]{1,0:T(8,128)} reduce(f32[4,2304,2048]{2,1,0:T(8,128)} %bitcast.13, f32[]{:T(128)} %constant.249.clone.1), dimensions={0}, to_apply=%region_25.26 | reduce | flops 14155776 | bytes 94371840 | tf_op jit(solution)/shard_map/reduce_sum | solution.py:153
  2158.5 30.4 %all-reduce = (f32[3,512]{1,0:T(4,128)}, f32[2048]{0:T(1024)}) all-reduce(f32[3,512]{1,0:T(4,128)S(1)} %convert_reduce_fusion.1, f32[2048]{0:T(1024)S(1)} %copy-done.21), channel_id=1, replica_groups=mesh['dp'=8,'tensor'=4] {'dp'}, use_global_device_ids=true, to_apply=%region_38.39 | all-reduce | flops 3584 | bytes 28672 | tf_op jit(solution)/shard_map/psum | solution.py:245
  2190.6 36.2 %reduce-scatter.8.cloned.1.call-done = bf16[3,256,512]{1,2,0:T(8,128)(2,1)} async-done(((bf16[3,2048,512]{1,2,0:T(8,128)(2,1)}), bf16[3,256,512]{1,2,0:T(8,128)(2,1)}) %reduce-scatter.8.cloned.1.call-update) | async-done | bytes 786448 | tf_op jit(solution)/shard_map/reduce_scatter | solution.py:232
  2229.4 87.7 %reduce-scatter.12.cloned.1.call-done = bf16[256,2048]{1,0:T(8,128)(2,1)} async-done(((bf16[2048,2048]{1,0:T(8,128)(2,1)}), bf16[256,2048]{1,0:T(8,128)(2,1)}) %reduce-scatter.12.cloned.1.call-update) | async-done | bytes 1048592 | tf_op jit(solution)/shard_map/reduce_scatter | solution.py:238
  2319.9 87.3 %reduce-scatter.14.cloned.1.call-done = bf16[2048,256]{1,0:T(8,128)(2,1)} async-done(((bf16[2048,2048]{1,0:T(8,128)(2,1)}), bf16[2048,256]{1,0:T(8,128)(2,1)}) %reduce-scatter.14.cloned.1.call-update) | async-done | bytes 1048592 | tf_op jit(solution)/shard_map/reduce_scatter | solution.py:241
  2409.9 132.8 %reduce-scatter.16.cloned.1.call-done = f32[64,3]{1,0:T(8,128)} async-done(((f32[2048,3]{1,0:T(8,128)}), f32[64,3]{1,0:T(8,128)}) %reduce-scatter.16.cloned.1.call-update) | async-done | bytes 784
  (246 shorter events, 586.2 us)
Async XLA Ops:
  7.2 4.7 copy-start.1
  7.2 6.6 copy-start.13
  7.2 6.6 copy-start.20
  7.2 70.9 %all-gather.11.cloned.1.call-start = ((), (), s32[]{:S(2)}) async-start(), calls=%async_computation.6 | async-start | bytes 7077888 | tf_op jit(solution)/shard_map/all_gather | solution.py:117
  9.7 164.8 %all-gather.9.cloned.1.call-start = ((), (), s32[]{:S(2)}) async-start(), calls=%async_computation.5 | async-start | bytes 11796480 | tf_op jit(solution)/shard_map/all_gather | solution.py:122
  16.2 158.4 %copy-start.24 = (f32[3,512]{1,0:T(4,128)S(1)}, f32[3,512]{1,0:T(4,128)}, u32[]{:S(2)}) copy-start(f32[3,512]{1,0:T(4,128)} %param.21) | copy-start | bytes 18436
  16.2 452.5 %all-gather.13.cloned.1.call-start = ((), (), s32[]{:S(2)}) async-start(), calls=%async_computation.7 | async-start | bytes 2359296 | tf_op jit(solution)/shard_map/all_gather | solution.py:118
  16.9 451.8 %all-gather.19.cloned.1.call-start = ((), (), s32[]{:S(2)}) async-start(), calls=%async_computation.10 | async-start | bytes 11796480 | tf_op jit(solution)/shard_map/all_gather | solution.py:168
  17.5 1167.5 %all-gather.15.cloned.1.call-start = ((), (), s32[]{:S(2)}) async-start(), calls=%async_computation.8 | async-start | bytes 9437184 | tf_op jit(solution)/shard_map/all_gather | solution.py:119
  18.1 1193.4 %all-gather.17.cloned.1.call-start = ((), (), s32[]{:S(2)}) async-start(), calls=%async_computation.9 | async-start | bytes 9437184 | tf_op jit(solution)/shard_map/all_gather | solution.py:120
  18.7 1449.3 %all-reduce.3.cloned.1.call-start = ((), (), s32[]{:S(2)}) async-start(), calls=%async_computation.11 | async-start | bytes 18874368 | tf_op jit(solution)/shard_map/psum | solution.py:246
  21.2 183.4 %copy-start.7 = (f32[2304,16]{0,1:T(8,128)}, f32[2304,16]{0,1:T(8,128)S(1)}, u32[]{:S(2)}) copy-start(f32[2304,16]{0,1:T(8,128)S(1)} %get-tuple-element.470) | copy-start | bytes 442372
  21.2 183.4 %copy-start.9 = (f32[2304,16]{0,1:T(8,128)}, f32[2304,16]{0,1:T(8,128)S(1)}, u32[]{:S(2)}) copy-start(f32[2304,16]{0,1:T(8,128)S(1)} %get-tuple-element.471) | copy-start | bytes 442372
  1136.6 12.4 copy-start.8
  1136.6 12.4 copy-start.10
  1145.1 3.9 copy-start
  1185.0 26.4 %copy-start.25 = (f32[2048]{0:T(1024)S(1)}, f32[2048]{0:T(1024)}, u32[]{:S(2)}) copy-start(f32[2048]{0:T(1024)} %param.24) | copy-start | bytes 24580
  1279.2 837.8 %all-gather.21.cloned.1.call-start = ((), (), s32[]{:S(2)}) async-start(), calls=%async_computation.16 | async-start | bytes 94371840 | tf_op jit(solution)/shard_map/all_gather | solution.py:154
  1326.8 9.6 copy-start.3
  1326.8 862.0 %reduce-scatter.10.cloned.1.call-start = ((), (), s32[]{:S(2)}) async-start(), calls=%async_computation.13 | async-start | bytes 2359296 | tf_op jit(solution)/shard_map/reduce_scatter | solution.py:235
  1336.3 890.5 %reduce-scatter.8.cloned.1.call-start = ((), (), s32[]{:S(2)}) async-start(), calls=%async_computation.12 | async-start | bytes 7077888 | tf_op jit(solution)/shard_map/reduce_scatter | solution.py:232
  1358.0 959.1 %reduce-scatter.12.cloned.1.call-start = ((), (), s32[]{:S(2)}) async-start(), calls=%async_computation.14 | async-start | bytes 9437184 | tf_op jit(solution)/shard_map/reduce_scatter | solution.py:238
  1384.7 1022.5 %reduce-scatter.14.cloned.1.call-start = ((), (), s32[]{:S(2)}) async-start(), calls=%async_computation.15 | async-start | bytes 9437184 | tf_op jit(solution)/shard_map/reduce_scatter | solution.py:241
  1415.9 52.1 %copy-start.2 = (bf16[576,2048]{1,0:T(8,128)(2,1)S(1)}, bf16[576,2048]{1,0:T(8,128)(2,1)}, u32[]{:S(2)}) copy-start(bf16[576,2048]{1,0:T(8,128)(2,1)} %param.16) | copy-start | bytes 7077892
  1415.9 52.1 %copy-start.12 = (f32[576]{0:T(1024)S(1)}, f32[576]{0:T(1024)}, u32[]{:S(2)}) copy-start(f32[576]{0:T(1024)} %copy-done.11) | copy-start | bytes 6916
  1415.9 52.1 %copy-start.14 = (f32[2048]{0:T(1024)S(1)}, f32[2048]{0:T(1024)}, u32[]{:S(2)}) copy-start(f32[2048]{0:T(1024)} %param.18) | copy-start | bytes 24580
  1415.9 1126.7 %reduce-scatter.16.cloned.1.call-start = ((), (), s32[]{:S(2)}) async-start(), calls=%async_computation.17 | async-start | bytes 1081344
  1433.4 37.3 %copy-start.18 = (f32[576]{0:T(1024)S(1)}, f32[576]{0:T(1024)}, u32[]{:S(2)}) copy-start(f32[576]{0:T(1024)} %copy-done.17) | copy-start | bytes 6916
  1433.4 37.3 %copy-start.16 = (f32[576]{0:T(1024)S(1)}, f32[576]{0:T(1024)}, u32[]{:S(2)}) copy-start(f32[576]{0:T(1024)} %copy-done.15) | copy-start | bytes 6916
  2117.0 31.3 %copy-start.19 = (f32[2048]{0:T(1024)S(1)}, f32[2048]{0:T(1024)}, u32[]{:S(2)}) copy-start(f32[2048]{0:T(1024)} %param.26) | copy-start | bytes 24580
  2148.3 9.3 copy-start.6
  2148.3 10.2 copy-start.21
  (8 other events, 12.8 us)
Sparse Core Ops, SparseCore 0:
  10.2 67.8 all-gather.10
  80.0 94.5 all-gather.8
  176.2 30.8 all-gather.12
  208.7 95.3 all-gather.18
  305.6 82.0 all-gather.14
  389.1 81.0 all-gather.16
  1279.3 188.6 all-reduce.2
  1469.9 647.0 all-gather.20
  2119.9 35.7 reduce-scatter.9
  2157.8 68.9 reduce-scatter.7
  2229.1 87.8 reduce-scatter.11
  2319.2 87.9 reduce-scatter.13
  2409.4 133.1 reduce-scatter.15
